TPU v7x, 32 devices: a whole 2x2x4 slice. The times are simulated.
32 devices in a mesh: pole: 4 (over x, core), row: 4 (over z), col: 2 (over y).
Axes of the slice: x: 2, y: 2, z: 4, core: 2. Of those that a mesh axis runs over, the one named last changes fastest.
Arguments:
- green: bfloat16 [4, 4096, 4096], P('pole', 'row', 'col'), may hold values from -6 to 6
- factor: bfloat16 [4, 4096, 1024], P('pole', 'row', 'col'), may hold values from -0.09375 to 0.09375
- diag_inverse: bfloat16 [4, 512, 1024], P('pole', 'row', 'col'), may hold values from -6 to 6
- pole_weight: float32 [4], P('pole'), may hold values from 0.25 to 1
- pattern: int32 [8, 2], replicated, may hold values 0 or 1
Outputs:
- off_density: float32 [4096, 1024], P(('row', 'pole'), 'col')
- diag_density: float32 [512, 1024], P(('pole', 'row'), 'col')
All inputs are finite; a program needn't handle non-finite values.
Results may differ from a plain program's by a relative error of at most 0.005.
Values may be sent and summed in bfloat16 or wider, within the bound.
No kernel may reach another device: no remote copies, remote signals or barrier semaphores. Data moves between devices by JAX's collectives and lax.ppermute only.
A program may use at most 64 MiB of HBM per device.

v0:
```python
import jax
import jax.numpy as jnp
from jax import lax
from jax.sharding import PartitionSpec as P

BLOCK = 512
ANC = 8


def body(green, factor, diag_inverse, pole_weight, pattern):
    poles_here = green.shape[0]
    local_rows = factor.shape[1]
    local_cols = factor.shape[2]
    level_count = pattern.shape[1]
    row_at = lax.axis_index("row")
    col_at = lax.axis_index("col")
    row_ids = (row_at * local_rows + jnp.arange(local_rows, dtype=jnp.int32)) // BLOCK
    col_ids = (col_at * local_cols + jnp.arange(local_cols, dtype=jnp.int32)) // BLOCK
    row_onehot = (row_ids[:, None] == jnp.arange(ANC, dtype=jnp.int32)[None, :]).astype(jnp.float32)
    col_onehot = (col_ids[:, None] == jnp.arange(level_count, dtype=jnp.int32)[None, :]).astype(
        jnp.float32
    )
    pattern_f = pattern.astype(jnp.float32)
    keep_mask = jnp.dot(jnp.dot(row_onehot, pattern_f), col_onehot.T)
    masked = factor * keep_mask.astype(jnp.bfloat16)[None]
    whole_rows = lax.all_gather(green, "col", axis=2, tiled=True)
    product = jnp.einsum(
        "pij,pjk->pik",
        whole_rows,
        lax.all_gather(masked, "row", axis=1, tiled=True),
        preferred_element_type=jnp.float32,
    )
    update = (product * keep_mask[None]).astype(jnp.bfloat16)
    weights = pole_weight[:, None, None]
    off_term = -jnp.sum(weights * update.astype(jnp.float32), axis=0)
    level_here = local_cols // BLOCK
    factor_split = masked.reshape(poles_here, local_rows, level_here, BLOCK)
    update_split = update.reshape(poles_here, local_rows, level_here, BLOCK)
    cross_term = jnp.einsum(
        "prka,prkb->pakb", factor_split, update_split, preferred_element_type=jnp.float32
    )
    cross_term = cross_term.reshape(poles_here, BLOCK, local_cols)
    diag_term = -jnp.sum(weights * cross_term, axis=0)
    dinv_count = diag_inverse.shape[1]
    dinv_rows = jnp.sum(weights * diag_inverse.astype(jnp.float32), axis=0)
    current = lax.dynamic_slice_in_dim(diag_term, row_at * dinv_count, dinv_count, 0)
    diag_term = lax.dynamic_update_slice_in_dim(
        diag_term, current + dinv_rows, row_at * dinv_count, 0
    )
    off_density, pole_part = (
        lax.psum_scatter(off_term, "pole", scatter_dimension=0, tiled=True),
        lax.psum_scatter(diag_term, "pole", scatter_dimension=0, tiled=True),
    )
    diag_density = lax.psum_scatter(pole_part, "row", scatter_dimension=0, tiled=True)
    return (off_density, diag_density)


def solution(mesh):
    in_specs = (
        P("pole", "row", "col"),
        P("pole", "row", "col"),
        P("pole", "row", "col"),
        P("pole"),
        P(),
    )
    out_specs = (P(("row", "pole"), "col"), P(("pole", "row"), "col"))
    return jax.shard_map(body, mesh=mesh, in_specs=in_specs, out_specs=out_specs, check_vma=False)
```

profile of v0, /device:TPU:0, one launch (start us, length us, event | category | flops | bytes accessed | tf_op | source)
XLA Modules:
  0.0 296.8 jit_solution(12370110417123104437)
XLA Ops:
  7.2 0.0 all-gather.3.cloned.1.call-start
  7.3 2.9 bitcast_multiply_fusion.1
  10.1 0.0 all-gather.3.cloned.1.call-update
  10.2 0.0 copy-start.2
  10.2 0.0 all-gather.5.cloned.1.call-start
  10.2 0.7 all-gather.5.cloned.1.call-update
  10.9 0.0 reduce-scatter.8.cloned.1.call-start
  11.6 0.0 copy-done.2
  11.6 0.1 copy.11
  11.8 82.0 %all-gather.3.cloned.1.call-done = bf16[1,4096,512]{2,1,0:T(8,128)(2,1)} async-done(((bf16[1,1024,512]{2,1,0:T(8,128)(2,1)}), bf16[1,4096,512]{2,1,0:T(8,128)(2,1)}) %all-gather.3.cloned.1.call-update) | async-done | bytes 4194320 | tf_op jit(solution)/shard_map/all_gather | solution.py:30
  93.8 104.0 %all-gather.5.cloned.1.call-done = bf16[1,1024,4096]{2,1,0:T(8,128)(2,1)} async-done(((bf16[1,1024,2048]{2,1,0:T(8,128)(2,1)}), bf16[1,1024,4096]{2,1,0:T(8,128)(2,1)}) %all-gather.5.cloned.1.call-update) | async-done | bytes 8388624 | tf_op jit(solution)/shard_map/all_gather | solution.py:26
  197.8 0.0 copy-start
  197.8 10.5 %multiply_negate_fusion = (f32[1024,512]{1,0:T(8,128)}, bf16[1024,512]{1,0:T(8,128)(2,1)S(1)}) fusion(f32[]{:T(128)} %bitcast.41, f32[1024,512]{1,0:T(8,128)S(1)} %get-tuple-element.7, bf16[1,4096,512]{2,1,0:T(8,128)(2,1)} %all-gather.3.cloned.1.call-done, bf16[1,1024,4096]{2,1,0:T(8,128)(2,1)} %all-gather.5.cloned.1.call-done), kind=kOutput, calls=%fused_computation.5 | convolution fusion | flops 4297588736 | bytes 17825796 | tf_op jit(solution)/shard_map/pij,pjk->pik/dot_general | solution.py:27
  208.3 0.0 copy-done
  208.3 0.7 fusion.8
  209.0 0.1 copy.16
  209.2 0.0 copy-start.1
  209.2 1.0 copy-done.1
  210.2 0.0 reduce-scatter.8.cloned.1.call-update
  210.2 0.0 reduce-scatter.10.cloned.1.call-start
  210.2 24.9 %reduce-scatter.8.cloned.1.call-done = f32[128,512]{0,1:T(8,128)} async-done(((f32[512,512]{0,1:T(8,128)}), f32[128,512]{0,1:T(8,128)}) %reduce-scatter.8.cloned.1.call-update) | async-done | bytes 262160 | tf_op jit(solution)/shard_map/reduce_scatter | solution.py:52
  235.2 1.8 copy.14
  236.9 0.0 reduce-scatter.10.cloned.1.call-update
  237.0 0.0 reduce-scatter.6.cloned.1.call-start
  237.0 0.5 reduce-scatter.6.cloned.1.call-update
  237.6 20.3 %reduce-scatter.10.cloned.1.call-done = f32[32,512]{1,0:T(8,128)} async-done(((f32[128,512]{1,0:T(8,128)}), f32[32,512]{1,0:T(8,128)}) %reduce-scatter.10.cloned.1.call-update) | async-done | bytes 65552
  257.9 32.4 %reduce-scatter.6.cloned.1.call-done = f32[256,512]{1,0:T(8,128)} async-done(((f32[1024,512]{1,0:T(8,128)}), f32[256,512]{1,0:T(8,128)}) %reduce-scatter.6.cloned.1.call-update) | async-done | bytes 524304 | tf_op jit(solution)/shard_map/reduce_scatter | solution.py:51
  (3 shorter events, 0.1 us)
Async XLA Ops:
  7.2 86.6 %all-gather.3.cloned.1.call-start = ((), (), s32[]{:S(2)}) async-start(), calls=%async_computation.3 | async-start | bytes 5242880 | tf_op jit(solution)/shard_map/all_gather | solution.py:30
  10.2 1.5 copy-start.2
  10.2 187.7 %all-gather.5.cloned.1.call-start = ((), (), s32[]{:S(2)}) async-start(), calls=%async_computation.4 | async-start | bytes 12582912 | tf_op jit(solution)/shard_map/all_gather | solution.py:26
  10.9 224.2 %reduce-scatter.8.cloned.1.call-start = ((), (), s32[]{:S(2)}) async-start(), calls=%async_computation.6 | async-start | bytes 1310720 | tf_op jit(solution)/shard_map/reduce_scatter | solution.py:52
  197.8 10.5 %copy-start = (bf16[1,1024,512]{2,1,0:T(8,128)(2,1)S(1)}, bf16[1,1024,512]{2,1,0:T(8,128)(2,1)}, u32[]{:S(2)}) copy-start(bf16[1,1024,512]{2,1,0:T(8,128)(2,1)} %get-tuple-element.6) | copy-start | bytes 3145732
  209.2 1.0 copy-start.1
  210.2 47.7 %reduce-scatter.10.cloned.1.call-start = ((), (), s32[]{:S(2)}) async-start(), calls=%async_computation.7 | async-start | bytes 327680
  237.0 53.3 %reduce-scatter.6.cloned.1.call-start = ((), (), s32[]{:S(2)}) async-start(), calls=%async_computation.5 | async-start | bytes 2621440 | tf_op jit(solution)/shard_map/reduce_scatter | solution.py:51
Sparse Core Ops, SparseCore 0:
  10.3 83.4 all-gather.2
  95.3 102.4 all-gather.4
  210.3 24.8 reduce-scatter.7
  237.8 19.9 reduce-scatter.9
  260.8 29.4 reduce-scatter.5
where the time goes:
time: 297 us
  waiting for transfers between devices  265 us (89%)
  between operations  14.5 us (5%)
  matrix products  14.1 us (5%)
    all_gather x1, waiting for transfers between devices, body(): whole_rows = lax.all_gather(green, 'col', axis=2, tiled=True)  104 us
    all_gather x1, waiting for transfers between devices, body(): lax.all_gather(masked, 'row', axis=1, tiled=True)  82 us
    reduce_scatter x1, waiting for transfers between devices, body(): lax.psum_scatter(off_term, 'pole', scatter_dimension=0, tiled=True)  32.4 us
    reduce_scatter x1, waiting for transfers between devices, body(): lax.psum_scatter(diag_term, 'pole', scatter_dimension=0, tiled=True)  24.9 us
    unnamed x6, waiting for transfers between devices  21.6 us
    dot_general x1, matrix products, body(): jnp.einsum('pij,pjk->pik', whole_rows, lax.all_gather(masked, 'row', axis...  10.5 us
  transfers between devices with their start and end apart: 5, of which 5 were waited for; matrix products, arithmetic and copies ran while one was open for 0% of the time, Pallas kernels for 0%

commit v1 on v0

--- a/solution.py
+++ b/solution.py
@@ -5,6 +5,22 @@
 
 BLOCK = 512
 ANC = 8
+
+
+def ring_gather(x, axis, dim):
+    ways, here, turn = (lax.axis_size(axis), lax.axis_index(axis), x.shape[dim])
+    shape = [n * ways if d == dim else n for d, n in enumerate(x.shape)]
+    full = lax.dynamic_update_slice_in_dim(jnp.zeros(shape, x.dtype), x, here * turn, axis=dim)
+    going_up = going_down = x
+    for far in range(1, ways // 2 + 1):
+        going_up = lax.ppermute(going_up, axis, [(d, (d + 1) % ways) for d in range(ways)])
+        full = lax.dynamic_update_slice_in_dim(full, going_up, (here - far) % ways * turn, axis=dim)
+        if 2 * far < ways:
+            going_down = lax.ppermute(going_down, axis, [(d, (d - 1) % ways) for d in range(ways)])
+            full = lax.dynamic_update_slice_in_dim(
+                full, going_down, (here + far) % ways * turn, axis=dim
+            )
+    return full
 
 
 def body(green, factor, diag_inverse, pole_weight, pattern):
@@ -27,7 +43,7 @@
     product = jnp.einsum(
         "pij,pjk->pik",
         whole_rows,
-        lax.all_gather(masked, "row", axis=1, tiled=True),
+        ring_gather(masked, "row", 1),
         preferred_element_type=jnp.float32,
     )
     update = (product * keep_mask[None]).astype(jnp.bfloat16)

time: 297 us -> 216 us (0.73)
  waiting for transfers between devices: 265 us -> 171 us
  local copies, waits for them, and re-layouts: 2.95 us -> 10.8 us
  starting transfers between devices: 0.2 us -> 5.16 us
    all_gather x1 -> x0, waiting for transfers between devices: 82 us -> none  [body(): lax.all_gather(masked, 'row', axis=1, tiled=True)]
    all_gather x1, waiting for transfers between devices: 104 us -> 28.2 us  [body(): whole_rows = lax.all_gather(green, 'col', axis=2, tiled=True)]
    ppermute x0 -> x3, waiting for transfers between devices: none -> 64.3 us  [the longest x2 44.9 us: ring_gather(): lax.ppermute(going_up, axis, [(d, (d + 1) % ways) for d in range(ways)])]
    dynamic_update_slice x0 -> x3, local copies, waits for them, and re-layouts: none -> 5.61 us  [the longest x2 3.36 us: ring_gather(): lax.dynamic_update_slice_in_dim(full, going_up, (here - far) % ways * tur...]
    ppermute x0 -> x3, starting transfers between devices: none -> 5 us  [the longest x2 2.96 us: ring_gather(): lax.ppermute(going_up, axis, [(d, (d + 1) % ways) for d in range(ways)])]
    unnamed x6 -> x5, waiting for transfers between devices: 21.6 us -> 21.7 us
  transfers between devices with their start and end apart: 5 -> 7, of which waited for: 5 -> 7; matrix products, arithmetic and copies ran while one was open for 0% -> 5% of each run, Pallas kernels for 0% -> 0%
where the time goes in v1:
time: 216 us; the launch traced here: 215 us
  waiting for transfers between devices  171 us (79%)
  between operations  14.5 us (7%)
  matrix products  13.3 us (6%)
  local copies, waits for them, and re-layouts  10.8 us (5%)
  starting transfers between devices  5.16 us (2%)
    ppermute x2, waiting for transfers between devices, ring_gather(): lax.ppermute(going_up, axis, [(d, (d + 1) % ways) for d in range(ways)])  44.9 us
    reduce_scatter x1, waiting for transfers between devices, body(): lax.psum_scatter(off_term, 'pole', scatter_dimension=0, tiled=True)  32.4 us
    all_gather x1, waiting for transfers between devices, body(): whole_rows = lax.all_gather(green, 'col', axis=2, tiled=True)  28.2 us
    reduce_scatter x1, waiting for transfers between devices, body(): lax.psum_scatter(diag_term, 'pole', scatter_dimension=0, tiled=True)  24.9 us
    unnamed x5, waiting for transfers between devices  21.7 us
    ppermute x1, waiting for transfers between devices, ring_gather(): lax.ppermute(going_down, axis, [(d, (d - 1) % ways) for d in range(ways)])  19.5 us
    dot_general x1, matrix products, body(): jnp.einsum('pij,pjk->pik', whole_rows, ring_gather(masked, 'row', 1), pre...  10.5 us
  transfers between devices with their start and end apart: 7, of which 7 were waited for; matrix products, arithmetic and copies ran while one was open for 5% of the time, Pallas kernels for 0%

profile of v1, /device:TPU:0, one launch (start us, length us, event | category | flops | bytes accessed | tf_op | source)
XLA Modules:
  0.0 215.4 jit_solution(11737593502819178949)
XLA Ops:
  7.2 0.0 copy-start.1
  7.2 0.0 copy-start.4
  7.2 0.0 all-gather.2.cloned.1.call-start
  7.2 0.7 all-gather.2.cloned.1.call-update
  7.9 0.0 reduce-scatter.8.cloned.1.call-start
  8.0 0.0 copy-start.3
  8.0 2.2 %broadcast.96 = bf16[4096,512]{1,0:T(8,128)(2,1)} broadcast(bf16[]{:T(256)} %constant.60.clone.1), dimensions={} | broadcast | bytes 4194306 | tf_op jit(solution)/shard_map/broadcast.33
  10.3 0.0 copy-done.1
  10.3 0.0 copy-done.4
  10.3 2.1 bitcast_dynamic-update-slice_fusion.3
  12.4 3.0 %collective-permute-start = (bf16[1,1024,512]{2,1,0:T(8,128)(2,1)}, bf16[1,1024,512]{2,1,0:T(8,128)(2,1)S(1)}, u32[]{:S(2)}, u32[]{:S(2)}) collective-permute-start(bf16[1,1024,512]{2,1,0:T(8,128)(2,1)} %get-tuple-element.7), channel_id=1, source_target_pairs={{0,2},{2,4},{4,6},{6,0},{1,3},{3,5},{5,7},{7,1},{8,10},{10,12},{12... | collective-permute-start | bytes 3145736 | tf_op jit(solution)/shard_map/ppermute | solution.py:16
  15.3 2.0 collective-permute-start.1
  17.4 24.3 %collective-permute-done = bf16[1,1024,512]{2,1,0:T(8,128)(2,1)S(1)} collective-permute-done((bf16[1,1024,512]{2,1,0:T(8,128)(2,1)}, bf16[1,1024,512]{2,1,0:T(8,128)(2,1)S(1)}, u32[]{:S(2)}, u32[]{:S(2)}) %collective-permute-start) | collective-permute-done | bytes 1048608 | tf_op jit(solution)/shard_map/ppermute | solution.py:16
  41.6 0.0 collective-permute-start.2
  42.3 0.0 copy-done.3
  42.3 0.1 copy.11
  42.4 1.1 bitcast_dynamic-update-slice_fusion.2
  43.5 19.5 %collective-permute-done.1 = bf16[1,1024,512]{2,1,0:T(8,128)(2,1)} collective-permute-done((bf16[1,1024,512]{2,1,0:T(8,128)(2,1)}, bf16[1,1024,512]{2,1,0:T(8,128)(2,1)}, u32[]{:S(2)}, u32[]{:S(2)}) %collective-permute-start.1) | collective-permute-done | bytes 1048608 | tf_op jit(solution)/shard_map/ppermute | solution.py:19
  63.0 2.3 %bitcast_dynamic-update-slice_fusion.1 = bf16[4096,512]{1,0:T(8,128)(2,1)} fusion(bf16[4096,512]{1,0:T(8,128)(2,1)} %bitcast_dynamic-update-slice_fusion.2, s32[]{:T(128)S(6)} %select_n.55, bf16[1,1024,512]{2,1,0:T(8,128)(2,1)} %collective-permute-done.1), kind=kLoop, calls=%fused_computation.10 | loop fusion | bytes 2097156 | tf_op jit(solution)/shard_map/dynamic_update_slice | solution.py:20
  65.2 20.6 %collective-permute-done.2 = bf16[1,1024,512]{2,1,0:T(8,128)(2,1)} collective-permute-done((bf16[1,1024,512]{2,1,0:T(8,128)(2,1)S(1)}, bf16[1,1024,512]{2,1,0:T(8,128)(2,1)}, u32[]{:S(2)}, u32[]{:S(2)}) %collective-permute-start.2) | collective-permute-done | bytes 1048608 | tf_op jit(solution)/shard_map/ppermute | solution.py:16
  85.8 2.3 %bitcast_dynamic-update-slice_fusion = bf16[4096,512]{1,0:T(8,128)(2,1)} fusion(bf16[4096,512]{1,0:T(8,128)(2,1)} %bitcast_dynamic-update-slice_fusion.1, s32[]{:T(128)S(6)} %select_n.57, bf16[1,1024,512]{2,1,0:T(8,128)(2,1)} %collective-permute-done.2), kind=kLoop, calls=%fused_computation.9 | loop fusion | bytes 2097156 | tf_op jit(solution)/shard_map/dynamic_update_slice | solution.py:17
  88.1 28.2 %all-gather.2.cloned.1.call-done = bf16[1,1024,4096]{2,1,0:T(8,128)(2,1)} async-done(((bf16[1,1024,2048]{2,1,0:T(8,128)(2,1)}), bf16[1,1024,4096]{2,1,0:T(8,128)(2,1)}) %all-gather.2.cloned.1.call-update) | async-done | bytes 8388624 | tf_op jit(solution)/shard_map/all_gather | solution.py:42
  116.3 0.0 copy-start.2
  116.3 10.5 %multiply_negate_fusion = (f32[1024,512]{1,0:T(8,128)}, bf16[1024,512]{1,0:T(8,128)(2,1)S(1)}) fusion(f32[]{:T(128)} %bitcast.43, f32[1024,512]{1,0:T(8,128)S(1)} %get-tuple-element.8, bf16[4096,512]{1,0:T(8,128)(2,1)} %bitcast_dynamic-update-slice_fusion, bf16[1,1024,4096]{2,1,0:T(8,128)(2,1)} %all-gather.2.cloned.1.call-done), kind=kOutput, calls=%fused_computation.4 | convolution fusion | flops 4297588736 | bytes 17825796 | tf_op jit(solution)/shard_map/pij,pjk->pik/dot_general | solution.py:43
  126.8 0.0 copy-done.2
  126.8 0.7 fusion.5
  127.5 0.1 copy.20
  127.7 0.0 copy-start
  127.7 1.0 copy-done
  128.6 0.0 reduce-scatter.8.cloned.1.call-update
  128.6 0.0 reduce-scatter.10.cloned.1.call-start
  128.7 24.9 %reduce-scatter.8.cloned.1.call-done = f32[128,512]{0,1:T(8,128)} async-done(((f32[512,512]{0,1:T(8,128)}), f32[128,512]{0,1:T(8,128)}) %reduce-scatter.8.cloned.1.call-update) | async-done | bytes 262160 | tf_op jit(solution)/shard_map/reduce_scatter | solution.py:68
  153.6 1.8 copy.14
  155.4 0.0 reduce-scatter.10.cloned.1.call-update
  155.4 0.0 reduce-scatter.6.cloned.1.call-start
  155.4 0.5 reduce-scatter.6.cloned.1.call-update
  156.0 20.5 %reduce-scatter.10.cloned.1.call-done = f32[32,512]{1,0:T(8,128)} async-done(((f32[128,512]{1,0:T(8,128)}), f32[32,512]{1,0:T(8,128)}) %reduce-scatter.10.cloned.1.call-update) | async-done | bytes 65552
  176.4 32.4 %reduce-scatter.6.cloned.1.call-done = f32[256,512]{1,0:T(8,128)} async-done(((f32[1024,512]{1,0:T(8,128)}), f32[256,512]{1,0:T(8,128)}) %reduce-scatter.6.cloned.1.call-update) | async-done | bytes 524304 | tf_op jit(solution)/shard_map/reduce_scatter | solution.py:67
  (3 shorter events, 0.1 us)
Async XLA Ops:
  7.2 3.1 %copy-start.1 = (bf16[1,1024,512]{2,1,0:T(8,128)(2,1)S(1)}, bf16[1,1024,512]{2,1,0:T(8,128)(2,1)}, u32[]{:S(2)}) copy-start(bf16[1,1024,512]{2,1,0:T(8,128)(2,1)} %param.6) | copy-start | bytes 3145732
  7.2 3.1 %copy-start.4 = (s32[8,2]{0,1:T(2,128)S(1)}, s32[8,2]{0,1:T(2,128)}, u32[]{:S(2)}) copy-start(s32[8,2]{0,1:T(2,128)} %param.9) | copy-start | bytes 196
  7.2 109.1 %all-gather.2.cloned.1.call-start = ((), (), s32[]{:S(2)}) async-start(), calls=%async_computation.3 | async-start | bytes 12582912 | tf_op jit(solution)/shard_map/all_gather | solution.py:42
  7.9 145.7 %reduce-scatter.8.cloned.1.call-start = ((), (), s32[]{:S(2)}) async-start(), calls=%async_computation.5 | async-start | bytes 1310720 | tf_op jit(solution)/shard_map/reduce_scatter | solution.py:68
  8.0 34.3 %copy-start.3 = (bf16[1,128,512]{2,1,0:T(8,128)(2,1)S(1)}, bf16[1,128,512]{2,1,0:T(8,128)(2,1)}, u32[]{:S(2)}) copy-start(bf16[1,128,512]{2,1,0:T(8,128)(2,1)} %param.7) | copy-start | bytes 393220
  12.4 29.3 %collective-permute-start = (bf16[1,1024,512]{2,1,0:T(8,128)(2,1)}, bf16[1,1024,512]{2,1,0:T(8,128)(2,1)S(1)}, u32[]{:S(2)}, u32[]{:S(2)}) collective-permute-start(bf16[1,1024,512]{2,1,0:T(8,128)(2,1)} %get-tuple-element.7), channel_id=1, source_target_pairs={{0,2},{2,4},{4,6},{6,0},{1,3},{3,5},{5,7},{7,1},{8,10},{10,12},{12... | collective-permute-start | bytes 3145736 | tf_op jit(solution)/shard_map/ppermute | solution.py:16
  15.3 47.6 %collective-permute-start.1 = (bf16[1,1024,512]{2,1,0:T(8,128)(2,1)}, bf16[1,1024,512]{2,1,0:T(8,128)(2,1)}, u32[]{:S(2)}, u32[]{:S(2)}) collective-permute-start(bf16[1,1024,512]{2,1,0:T(8,128)(2,1)} %get-tuple-element.7), channel_id=1, source_target_pairs={{0,6},{2,0},{4,2},{6,4},{1,7},{3,1},{5,3},{7,5},{8,14},{10,8},{12,... | collective-permute-start | bytes 3145736 | tf_op jit(solution)/shard_map/ppermute | solution.py:19
  41.6 44.2 %collective-permute-start.2 = (bf16[1,1024,512]{2,1,0:T(8,128)(2,1)S(1)}, bf16[1,1024,512]{2,1,0:T(8,128)(2,1)}, u32[]{:S(2)}, u32[]{:S(2)}) collective-permute-start(bf16[1,1024,512]{2,1,0:T(8,128)(2,1)S(1)} %collective-permute-done), channel_id=1, source_target_pairs={{0,2},{2,4},{4,6},{6,0},{1,3},{3,5},{5,7},{7,1},{8,10},{10,12},{12... | collective-permute-start | bytes 3145736 | tf_op jit(solution)/shard_map/ppermute | solution.py:16
  116.3 10.5 %copy-start.2 = (bf16[1,1024,512]{2,1,0:T(8,128)(2,1)S(1)}, bf16[1,1024,512]{2,1,0:T(8,128)(2,1)}, u32[]{:S(2)}) copy-start(bf16[1,1024,512]{2,1,0:T(8,128)(2,1)} %get-tuple-element.7) | copy-start | bytes 3145732
  127.7 1.0 copy-start
  128.6 47.8 %reduce-scatter.10.cloned.1.call-start = ((), (), s32[]{:S(2)}) async-start(), calls=%async_computation.6 | async-start | bytes 327680
  155.4 53.4 %reduce-scatter.6.cloned.1.call-start = ((), (), s32[]{:S(2)}) async-start(), calls=%async_computation.4 | async-start | bytes 2621440 | tf_op jit(solution)/shard_map/reduce_scatter | solution.py:67
Sparse Core Ops, SparseCore 0:
  9.5 106.6 all-gather.1
  128.8 24.7 reduce-scatter.7
  156.4 19.9 reduce-scatter.9
  179.4 29.3 reduce-scatter.5
